TPU v7x, 32 devices: a whole 2x2x4 slice. The times are simulated.
32 devices in a mesh: frame: 16 (over z, y, x), row: 2 (over core).
Axes of the slice: x: 2, y: 2, z: 4, core: 2. Of those that a mesh axis runs over, the one named last changes fastest.
Arguments:
- tokens: bfloat16 [16, 2, 128, 2048], P('frame', 'row'), may hold values from -6 to 6
- cotangent: bfloat16 [16, 2, 128, 2048], P('frame', 'row'), may hold values from -6 to 6
- timestep: int32 [1], replicated, may hold values from 0 to 999
- mod_weight: bfloat16 [256, 4096], P(None, 'frame'), may hold values from -0.375 to 0.375
- proj_weight: bfloat16 [2048, 256], P('frame'), may hold values from -0.125 to 0.125
- step_weight: bfloat16 [2048, 32], P('frame'), may hold values from -0.125 to 0.125
- step_bias: float32 [32], replicated, may hold values from -1 to 1
- rate_space: float32 [32], replicated, may hold values from 0.001171875 to 0.05
- rate_time: float32 [32], replicated, may hold values from 0.01875 to 1
- skip_gain: float32 [32], replicated, may hold values from 0.5 to 1.5
Outputs:
- mixed: bfloat16 [16, 2, 128, 2048], P('frame', 'row')
- d_tokens: bfloat16 [16, 2, 128, 2048], P('frame', 'row')
- grad_proj: float32 [2048, 256], P('frame')
- grad_step: float32 [2048, 32], P('frame')
- grad_mod: float32 [256, 4096], P(None, 'frame')
All inputs are finite; a program needn't handle non-finite values.
Results may differ from a plain program's by a relative error of at most 0.015.
Values may be sent and summed in bfloat16 or wider, within the bound.
No kernel may reach another device: no remote copies, remote signals or barrier semaphores. Data moves between devices by JAX's collectives and lax.ppermute only.
A program may use at most 64 MiB of HBM per device.

v0:
```python
import math
import jax
import jax.numpy as jnp
from jax import lax
from jax.sharding import PartitionSpec as P

norm_eps = 1e-05


def prefix(array, axis, join, neutral):
    place = lax.axis_index(axis)
    gathered = jax.tree.map(
        lambda a, kind: lax.all_gather(a.astype(kind), axis), array, (jnp.bfloat16, jnp.bfloat16)
    )
    state = jax.tree.map(lambda a, e: jnp.zeros_like(a) + jnp.asarray(e, a.dtype), array, neutral)

    def prefix_one(hop, state):
        return join(
            state,
            jax.tree.map(
                lambda a, own: lax.dynamic_index_in_dim(a, hop, 0, False).astype(own.dtype),
                gathered,
                array,
            ),
        )

    return lax.fori_loop(0, place, prefix_one, state)


def carried_in(array, axis, join, neutral):
    count = lax.axis_size(axis)
    place = lax.axis_index(axis)
    ahead = count - 1 - place
    gathered = jax.tree.map(
        lambda a, kind: lax.all_gather(a.astype(kind), axis),
        array,
        jax.tree.map(lambda a: jnp.bfloat16 if a.dtype == jnp.float32 else a.dtype, array),
    )
    state = jax.tree.map(lambda a, e: jnp.zeros_like(a) + jnp.asarray(e, a.dtype), array, neutral)

    def carried_one(hop, state):
        source = count - 1 - hop
        return join(
            state,
            jax.tree.map(
                lambda a, own: lax.dynamic_index_in_dim(a, source, 0, False).astype(own.dtype),
                gathered,
                array,
            ),
        )

    return lax.fori_loop(0, ahead, carried_one, state)


def time_embed(timestep, embed_dim):
    half_dim = embed_dim // 2
    frequency = jnp.exp(-math.log(10000.0) * jnp.arange(half_dim, dtype=jnp.float32) / half_dim)
    angles = timestep.astype(jnp.float32)[:, None] * frequency[None, :]
    return jax.nn.silu(jnp.concatenate([jnp.cos(angles), jnp.sin(angles)], axis=1))


def normalize(values):
    return values * lax.rsqrt(jnp.mean(values * values, axis=-1, keepdims=True) + norm_eps)


def block_parts(normed, coeffs, logits, step_bias, decay_rate, need_end):
    seq_count, length, feat_width = normed.shape
    head_count = decay_rate.shape[0]
    inputs = normed.reshape(seq_count, length, head_count, feat_width // head_count)
    state_size = coeffs.shape[-1] // 2
    b_part = coeffs[..., :state_size]
    c_part = coeffs[..., state_size:]
    step_size = jax.nn.softplus(logits.astype(jnp.float32) + step_bias)
    cum_log = jnp.cumsum(-step_size * decay_rate, axis=1)
    scores = (
        jnp.einsum("stn,sun->stu", c_part, b_part, preferred_element_type=jnp.float32) / state_size
    )
    lag_rows = jnp.swapaxes(cum_log, 1, 2)
    causal = jnp.tril(jnp.ones((length, length), dtype=bool))
    differences = lag_rows[:, :, :, None] - lag_rows[:, :, None, :]
    decays = jnp.where(causal, jnp.exp(jnp.where(causal, differences, 0.0)), 0.0)
    spread = jnp.swapaxes(step_size, 1, 2)
    weights = (scores[:, None, :, :] * decays * spread[:, :, None, :]).astype(jnp.bfloat16)
    inner_out = jnp.einsum("shtu,suhp->sthp", weights, inputs, preferred_element_type=jnp.float32)
    inner_out = inner_out.reshape(seq_count, length, feat_width)
    if need_end:
        end_log = cum_log[:, -1:, :]
        lead_decay = jnp.exp(end_log - cum_log) * step_size
        scaled = (inputs.astype(jnp.float32) * lead_decay[..., None]).astype(jnp.bfloat16)
        end_local = jnp.einsum("sthp,stn->shpn", scaled, b_part, preferred_element_type=jnp.float32)
    else:
        end_local = jnp.zeros(
            (seq_count, head_count, feat_width // head_count, state_size), jnp.float32
        )
    return (inner_out, end_local, cum_log, c_part)


def carry_term(cum_log, c_part, state_in):
    seq_count, length, head_count = cum_log.shape
    state_size = c_part.shape[-1]
    reached = jnp.einsum(
        "stn,shpn->sthp", c_part.astype(jnp.float32), state_in, precision=lax.Precision.HIGHEST
    )
    return (reached * jnp.exp(cum_log)[..., None] / state_size).reshape(seq_count, length, -1)


def combine_forward(earlier, later):
    return (earlier[0] * later[0], later[0][:, :, None, None] * earlier[1] + later[1])


def combine_backward(earlier, later):
    return (earlier[0] * later[0], later[1] + later[0][:, :, None, None] * earlier[1])


def per_device(
    tokens,
    cotangent,
    timestep,
    mod_weight,
    proj_weight,
    step_weight,
    step_bias,
    rate_space,
    rate_time,
    skip_gain,
):
    frame_count = lax.axis_size("frame")
    row_count = lax.axis_size("row")
    frame_id = lax.axis_index("frame")
    feat_width = tokens.shape[-1]
    band_len = tokens.shape[1] * tokens.shape[2]
    clip_count = timestep.shape[0]
    clip_frames = frame_count // clip_count
    site_count = band_len // frame_count
    head_count = rate_space.shape[0]
    clip_id = frame_id // clip_frames
    factor = (frame_count * row_count * band_len) ** (-0.5)
    activated = time_embed(timestep, mod_weight.shape[0]).astype(jnp.bfloat16)
    proj_full, step_full = (
        lax.all_gather(proj_weight, "frame", axis=0, tiled=True),
        lax.all_gather(step_weight, "frame", axis=0, tiled=True),
    )
    mod_full = lax.all_gather(mod_weight, "frame", axis=1, tiled=True)
    modulation = jnp.dot(activated, mod_full, preferred_element_type=jnp.float32)
    clip_mod = lax.dynamic_index_in_dim(modulation, clip_id, 0, keepdims=False)
    shift_vec = clip_mod[:feat_width]
    scale_vec = clip_mod[feat_width:]
    tokens_wide = tokens.reshape(band_len, feat_width).astype(jnp.float32)
    unit_rows = normalize(tokens_wide)
    normed = (unit_rows * (1.0 + scale_vec) + shift_vec).astype(jnp.bfloat16)
    projected = jnp.dot(normed, proj_full, preferred_element_type=jnp.float32).astype(jnp.bfloat16)
    logits = jnp.dot(normed, step_full, preferred_element_type=jnp.float32).astype(jnp.bfloat16)
    skip_full = jnp.repeat(skip_gain, feat_width // head_count)
    flat_grad = cotangent.reshape(band_len, feat_width)

    def space_parts(normed_band, proj_band, logit_band):
        return block_parts(normed_band, proj_band, logit_band, step_bias, rate_space, True)

    parts_out, parts_pull = jax.vjp(space_parts, normed[None], projected[None], logits[None])
    inner_out, end_local, cum_log, c_part = parts_out
    end_decay = jnp.exp(cum_log[:, -1, :])
    identity = (jnp.ones_like(end_decay), jnp.zeros_like(end_local))
    prefix_decay, state_in = prefix((end_decay, end_local), "row", combine_forward, identity)
    carried, carry_pull = jax.vjp(carry_term, cum_log, c_part, state_in)
    space_out = (inner_out + carried)[0]
    site_normed, site_grad = (
        lax.all_to_all(normed, "frame", split_axis=0, concat_axis=0, tiled=True),
        lax.all_to_all(flat_grad, "frame", split_axis=0, concat_axis=0, tiled=True),
    )
    site_proj = jnp.dot(site_normed, proj_full, preferred_element_type=jnp.float32).astype(
        jnp.bfloat16
    )
    site_logits = jnp.dot(site_normed, step_full, preferred_element_type=jnp.float32).astype(
        jnp.bfloat16
    )

    def to_seq(member):
        shaped = member.reshape(frame_count, site_count, member.shape[-1])
        return shaped.transpose(1, 0, 2)

    def from_seq(member):
        return member.transpose(1, 0, 2).reshape(frame_count * site_count, member.shape[-1])

    def time_path(normed_seq, proj_seq, logit_seq):
        return block_parts(normed_seq, proj_seq, logit_seq, step_bias, rate_time, False)[0]

    time_out, time_pull = jax.vjp(
        time_path, to_seq(site_normed), to_seq(site_proj), to_seq(site_logits)
    )
    time_low = from_seq(time_out.astype(jnp.bfloat16))
    time_dnorm, time_dproj, time_dlogit = time_pull(to_seq(site_grad).astype(jnp.float32))
    site_dproj = from_seq(time_dproj)
    site_dlogit = from_seq(time_dlogit)
    site_back = (
        from_seq(time_dnorm).astype(jnp.float32)
        + jnp.dot(site_dproj, proj_full.T, preferred_element_type=jnp.float32)
        + jnp.dot(site_dlogit, step_full.T, preferred_element_type=jnp.float32)
    ).astype(jnp.bfloat16)
    proj_time = jnp.dot(site_normed.T, site_dproj, preferred_element_type=jnp.float32)
    step_time = jnp.dot(site_normed.T, site_dlogit, preferred_element_type=jnp.float32)
    space_time, time_back = (
        lax.all_to_all(time_low, "frame", split_axis=0, concat_axis=0, tiled=True),
        lax.all_to_all(site_back, "frame", split_axis=0, concat_axis=0, tiled=True),
    )
    mixed = (
        space_out + space_time.astype(jnp.float32) + skip_full * normed.astype(jnp.float32)
    ).astype(jnp.bfloat16)
    upstream = flat_grad.astype(jnp.float32)
    carry_dcum, carry_dc, own_state = carry_pull(upstream[None])
    suffix_decay, later_grad = carried_in((end_decay, own_state), "row", combine_backward, identity)
    end_dlog = jnp.sum(later_grad * state_in, axis=(2, 3)) * end_decay
    carry_dcum = carry_dcum.at[:, -1, :].add(end_dlog)
    space_dnorm, space_dproj, space_dlogit = parts_pull(
        (upstream[None], later_grad, carry_dcum, carry_dc)
    )
    skip_dnorm = (upstream * skip_full).astype(jnp.bfloat16)
    total_dnorm = space_dnorm[0] + skip_dnorm
    pre_grad = (
        total_dnorm.astype(jnp.float32)
        + jnp.dot(space_dproj[0], proj_full.T, preferred_element_type=jnp.float32)
        + jnp.dot(space_dlogit[0], step_full.T, preferred_element_type=jnp.float32)
        + time_back.astype(jnp.float32)
    )
    proj_term = jnp.dot(normed.T, space_dproj[0], preferred_element_type=jnp.float32) + proj_time
    step_term = jnp.dot(normed.T, space_dlogit[0], preferred_element_type=jnp.float32) + step_time
    shift_grad = jnp.sum(pre_grad, axis=0)
    scale_grad = jnp.sum(pre_grad * unit_rows, axis=0)
    picked = (jnp.arange(clip_count) == clip_id).astype(jnp.float32)
    mod_term = jnp.concatenate([shift_grad, scale_grad])[:, None] * picked[None, :]
    proj_sum, step_sum, mod_sum = (
        lax.psum(proj_term.astype(jnp.bfloat16), "row").astype(jnp.float32),
        lax.psum(step_term.astype(jnp.bfloat16), "row").astype(jnp.float32),
        lax.psum(mod_term.astype(jnp.bfloat16), "row").astype(jnp.float32),
    )
    proj_sum, step_sum, mod_sum = (
        lax.psum_scatter(proj_sum, "frame", scatter_dimension=0, tiled=True),
        lax.psum_scatter(step_sum, "frame", scatter_dimension=0, tiled=True),
        lax.psum_scatter(mod_sum, "frame", scatter_dimension=0, tiled=True),
    )
    grad_proj = proj_sum * factor
    grad_step = step_sum * factor
    grad_mod = (
        jnp.dot(activated.astype(jnp.float32).T, mod_sum.T, precision=lax.Precision.HIGHEST)
        * factor
    )
    unused, norm_pull = jax.vjp(normalize, tokens_wide)
    (tokens_grad,) = norm_pull(pre_grad * (1.0 + scale_vec))
    d_tokens = tokens_grad.astype(jnp.bfloat16).reshape(tokens.shape)
    return (mixed.reshape(tokens.shape), d_tokens, grad_proj, grad_step, grad_mod)


def solution(mesh):
    placed = (
        P("frame", "row", None, None),
        P("frame", "row", None, None),
        P(),
        P(None, "frame"),
        P("frame", None),
        P("frame", None),
        P(),
        P(),
        P(),
        P(),
    )
    return jax.shard_map(
        per_device,
        mesh=mesh,
        in_specs=placed,
        out_specs=(
            P("frame", "row", None, None),
            P("frame", "row", None, None),
            P("frame", None),
            P("frame", None),
            P(None, "frame"),
        ),
        check_vma=False,
    )
```

profile of v0, /device:TPU:0, one launch (start us, length us, event | category | flops | bytes accessed | tf_op | source)
XLA Modules:
  0.0 490.7 jit_solution(3879071118985589353)
XLA Ops:
  7.9 8.4 %all-to-all-start.2 = ((bf16[16,8,2048]{2,1,0:T(8,128)(2,1)}), bf16[16,8,2048]{2,1,0:T(8,128)(2,1)S(1)}, u32[]{:S(2)}, u32[]{:S(2)}) async-start(bf16[16,8,2048]{2,1,0:T(8,128)(2,1)} %bitcast.449), calls=%async_computation.2 | async-start | bytes 1048576 | tf_op jit(solution)/shard_map/all_to_all | solution.py:168
  17.0 2.0 copy.217
  20.4 1.2 copy.191
  22.7 42.0 %all_gather.29 = bf16[2048,32]{0,1:T(8,128)(2,1)S(1)} all-gather(bf16[128,32]{0,1:T(8,128)(2,1)S(1)} %copy-done.52), channel_id=1, replica_groups=mesh['frame'=16,'row'=2] {'frame'}, dimensions={0}, use_global_device_ids=true | all-gather | bytes 139264 | tf_op jit(solution)/shard_map/all_gather | solution.py:141
  65.8 2.1 reshape.933
  67.9 12.4 %all-gather.7.cloned.1.call-done = bf16[256,4096]{1,0:T(8,128)(2,1)} async-done(((bf16[256,256]{1,0:T(8,128)(2,1)}), bf16[256,4096]{1,0:T(8,128)(2,1)}) %all-gather.7.cloned.1.call-update) | async-done | bytes 2097168 | tf_op jit(solution)/shard_map/all_gather | solution.py:143
  80.3 2.0 fusion.182
  83.1 1.3 copy.213
  84.4 1.0 fusion.62
  85.5 4.0 all-to-all-start
  89.5 2.5 convert_multiply_fusion
  93.3 1.5 copy.214
  94.9 42.8 %all-gather.9.cloned.1.call-done = bf16[2048,256]{1,0:T(8,128)(2,1)} async-done(((bf16[128,256]{1,0:T(8,128)(2,1)}), bf16[2048,256]{1,0:T(8,128)(2,1)}) %all-gather.9.cloned.1.call-update) | async-done | bytes 1048592 | tf_op jit(solution)/shard_map/all_gather | solution.py:140
  137.7 1.6 fusion.33
  139.3 1.4 convolution_convert_fusion.5
  141.2 2.1 all_gather.30
  143.4 1.3 copy.223
  150.6 1.1 reshape.936
  151.7 3.2 convert_bitcast_fusion
  155.0 3.5 fusion.26
  160.1 2.0 copy.231
  162.0 2.1 reshape.922
  164.1 1.6 copy.237
  165.7 1.6 copy.236
  171.0 1.1 fusion.3
  172.1 4.5 all-to-all-start.3
  176.8 1.4 while.28
  176.9 1.4 convert_add_fusion.6
  178.3 2.1 multiply_reduce_fusion.2
  181.2 1.9 fusion.177
  183.2 1.1 mul.537
  184.3 1.6 copy.197
  185.8 1.7 fusion.50
  187.5 1.3 copy.198
  188.8 1.1 convolution_convert_fusion.7
  190.0 2.7 convolution_bitcast_fusion
  195.5 3.8 fusion.24
  204.2 2.4 fusion.35
  206.6 2.2 multiply_reduce_fusion.1
  211.4 1.1 reduce_window_sum.49
  213.5 2.0 fusion.4
  215.7 2.4 fusion
  218.2 2.3 fusion.32
  221.6 1.5 convolution_add_fusion.4
  223.1 2.6 fusion.70
  225.8 4.2 psum.23
  230.0 1.8 copy.246
  231.8 7.7 %all-reduce.8.cloned.1.call-done = (bf16[2048,256]{1,0:T(8,128)(2,1)}, bf16[2048,32]{0,1:T(8,128)(2,1)}) async-done(((bf16[2048,256]{1,0:T(8,128)(2,1)}, bf16[2048,32]{0,1:T(8,128)(2,1)}), (bf16[2048,256]{1,0:T(8,128)(2,1)}, bf16[2048,32]{0,1:T(8,128)(2,1)})) %all-reduce.8.cloned.1.call-update) | async-done | bytes 1179664 | tf_op jit(solution)/shard_map/psum | solution.py:231
  239.5 1.6 convert_element_type.535
  241.3 2.8 convert_element_type.533
  244.2 1.3 fusion.27
  246.6 1.1 copy.211
  247.7 6.8 %all-to-all-start.1 = ((bf16[16,8,2048]{2,1,0:T(8,128)(2,1)}), bf16[16,8,2048]{2,1,0:T(8,128)(2,1)S(1)}, u32[]{:S(2)}, u32[]{:S(2)}) async-start(bf16[16,8,2048]{2,1,0:T(8,128)(2,1)} %copy.211), calls=%async_computation.1 | async-start | bytes 1048576 | tf_op jit(solution)/shard_map/all_to_all | solution.py:202
  254.6 2.8 fusion.80
  257.4 2.7 copy.201
  260.1 1.3 copy.202
  261.5 1.1 fusion.81
  262.6 10.8 %all-to-all-done.1 = bf16[16,8,2048]{2,1,0:T(8,128)(2,1)S(1)} async-done(((bf16[16,8,2048]{2,1,0:T(8,128)(2,1)}), bf16[16,8,2048]{2,1,0:T(8,128)(2,1)S(1)}, u32[]{:S(2)}, u32[]{:S(2)}) %all-to-all-start.1) | async-done | bytes 524320 | tf_op jit(solution)/shard_map/all_to_all | solution.py:202
  273.4 2.4 fusion.52
  275.8 50.2 %reduce-scatter.10.cloned.1.call-done = f32[256,1]{1,0:T(8,128)} async-done(((f32[4096,1]{1,0:T(8,128)}), f32[256,1]{1,0:T(8,128)}) %reduce-scatter.10.cloned.1.call-update) | async-done | bytes 1040
  327.7 74.5 %reduce-scatter.8.cloned.1.call-done = f32[128,32]{0,1:T(8,128)} async-done(((f32[2048,32]{0,1:T(8,128)}), f32[128,32]{0,1:T(8,128)}) %reduce-scatter.8.cloned.1.call-update) | async-done | bytes 16400 | tf_op jit(solution)/shard_map/reduce_scatter | solution.py:237
  402.2 1.3 broadcast_multiply_fusion.2
  403.6 78.7 %reduce-scatter.6.cloned.1.call-done = f32[128,256]{1,0:T(8,128)} async-done(((f32[2048,256]{1,0:T(8,128)}), f32[128,256]{1,0:T(8,128)}) %reduce-scatter.6.cloned.1.call-update) | async-done | bytes 131088 | tf_op jit(solution)/shard_map/reduce_scatter | solution.py:236
  482.3 1.6 broadcast_multiply_fusion
  (213 shorter events, 34.6 us)
Async XLA Ops:
  7.2 13.2 %copy-start = (bf16[1,1,128,2048]{3,2,1,0:T(8,128)(2,1)S(1)}, bf16[1,1,128,2048]{3,2,1,0:T(8,128)(2,1)}, u32[]{:S(2)}) copy-start(bf16[1,1,128,2048]{3,2,1,0:T(8,128)(2,1)} %param.16) | copy-start | bytes 1572868
  7.2 14.5 %copy-start.60 = (f32[32]{0:T(128)S(1)}, f32[32]{0:T(128)}, u32[]{:S(2)}) copy-start(f32[32]{0:T(128)} %param.25) | copy-start | bytes 388
  7.2 73.2 %all-gather.7.cloned.1.call-start = ((), (), s32[]{:S(2)}) async-start(), calls=%async_computation.7 | async-start | bytes 2228224 | tf_op jit(solution)/shard_map/all_gather | solution.py:143
  7.9 14.8 %copy-start.52 = (bf16[128,32]{0,1:T(8,128)(2,1)S(1)}, bf16[128,32]{0,1:T(8,128)(2,1)}, u32[]{:S(2)}) copy-start(bf16[128,32]{0,1:T(8,128)(2,1)} %param.21) | copy-start | bytes 24580
  7.9 57.9 %all-to-all-start.2 = ((bf16[16,8,2048]{2,1,0:T(8,128)(2,1)}), bf16[16,8,2048]{2,1,0:T(8,128)(2,1)S(1)}, u32[]{:S(2)}, u32[]{:S(2)}) async-start(bf16[16,8,2048]{2,1,0:T(8,128)(2,1)} %bitcast.449), calls=%async_computation.2 | async-start | bytes 1048576 | tf_op jit(solution)/shard_map/all_to_all | solution.py:168
  16.3 121.4 %all-gather.9.cloned.1.call-start = ((), (), s32[]{:S(2)}) async-start(), calls=%async_computation.8 | async-start | bytes 1114112 | tf_op jit(solution)/shard_map/all_gather | solution.py:140
  22.4 59.9 %copy-start.53 = (f32[32]{0:T(128)S(1)}, f32[32]{0:T(128)}, u32[]{:S(2)}) copy-start(f32[32]{0:T(128)} %param.22) | copy-start | bytes 388
  22.6 60.1 %copy-start.58 = (f32[128]{0:T(128)}, f32[128]{0:T(128)S(1)}, u32[]{:S(2)}) copy-start(f32[128]{0:T(128)S(1)} %fusion.74) | copy-start | bytes 1540
  22.6 115.1 %copy-start.45 = (f32[128]{0:T(128)}, f32[128]{0:T(128)S(1)}, u32[]{:S(2)}) copy-start(f32[128]{0:T(128)S(1)} %fusion.158) | copy-start | bytes 1540
  67.9 14.8 %copy-start.55 = (f32[32]{0:T(128)S(1)}, f32[32]{0:T(128)}, u32[]{:S(2)}) copy-start(f32[32]{0:T(128)} %param.23) | copy-start | bytes 388
  83.1 6.4 %copy-start.5 = (bf16[1,1,128,2048]{3,2,1,0:T(8,128)(2,1)S(1)}, bf16[1,1,128,2048]{3,2,1,0:T(8,128)(2,1)}, u32[]{:S(2)}) copy-start(bf16[1,1,128,2048]{3,2,1,0:T(8,128)(2,1)} %param.17) | copy-start | bytes 1572868
  85.5 60.6 %all-to-all-start = ((bf16[16,8,2048]{2,1,0:T(8,128)(2,1)}), bf16[16,8,2048]{2,1,0:T(8,128)(2,1)S(1)}, u32[]{:S(2)}, u32[]{:S(2)}) async-start(bf16[16,8,2048]{2,1,0:T(8,128)(2,1)} %fusion.62), calls=%async_computation | async-start | bytes 1048576 | tf_op jit(solution)/shard_map/all_to_all | solution.py:167
  89.5 87.2 %all-gather.13.cloned.1.call-start = ((), (), s32[]{:S(2)}) async-start(), calls=%async_computation.12 | async-start | bytes 1572864 | tf_op jit(solution)/shard_map/all_gather | solution.py:35
  94.9 45.8 %copy-start.3 = (f32[1,1,128,2048]{2,3,1,0:T(8,128)}, f32[1,1,128,2048]{2,3,1,0:T(8,128)S(1)}, u32[]{:S(2)}) copy-start(f32[1,1,128,2048]{2,3,1,0:T(8,128)S(1)} %copy.214) | copy-start | bytes 3145732
  140.7 8.8 %copy-start.1 = (bf16[2048,256]{1,0:T(8,128)(2,1)S(1)}, bf16[2048,256]{1,0:T(8,128)(2,1)}, u32[]{:S(2)}) copy-start(bf16[2048,256]{1,0:T(8,128)(2,1)} %all-gather.9.cloned.1.call-done) | copy-start | bytes 3145732
  151.7 3.3 copy-start.14
  151.7 3.3 copy-start.16
  151.7 3.3 copy-start.31
  151.7 3.3 copy-start.33
  151.7 3.3 copy-start.43
  151.7 3.3 copy-start.56
  155.0 4.2 copy-start.18
  171.0 5.8 %copy-start.61 = (bf16[2,1,32]{2,1,0:T(2,128)(2,1)S(1)}, bf16[2,1,32]{2,1,0:T(2,128)(2,1)}, u32[]{:S(2)}) copy-start(bf16[2,1,32]{2,1,0:T(2,128)(2,1)} %all_gather.30) | copy-start | bytes 388
  172.1 51.0 %all-to-all-start.3 = ((bf16[16,8,2048]{2,1,0:T(8,128)(2,1)}), bf16[16,8,2048]{2,1,0:T(8,128)(2,1)}, u32[]{:S(2)}, u32[]{:S(2)}) async-start(bf16[16,8,2048]{2,1,0:T(8,128)(2,1)} %fusion.3), calls=%async_computation.3 | async-start | bytes 1048576 | tf_op jit(solution)/shard_map/all_to_all | solution.py:203
  176.6 26.0 %all-gather.11.cloned.1.call-start = ((), (), s32[]{:S(2)}) async-start(), calls=%async_computation.11 | async-start | bytes 1572864 | tf_op jit(solution)/shard_map/all_gather | solution.py:13
  189.9 5.6 %copy-start.19 = (bf16[1,1,128,2048]{2,3,1,0:T(8,128)(2,1)S(1)}, bf16[1,1,128,2048]{2,3,1,0:T(8,128)(2,1)}, u32[]{:S(2)}) copy-start(bf16[1,1,128,2048]{2,3,1,0:T(8,128)(2,1)} %copy.217) | copy-start | bytes 1572868
  189.9 49.6 %all-reduce.8.cloned.1.call-start = ((), (), s32[]{:S(2)}) async-start(), calls=%async_computation.14 | async-start | bytes 2359296 | tf_op jit(solution)/shard_map/psum | solution.py:231
  190.0 2.7 copy-start.23
  195.5 3.8 copy-start.49
  199.3 3.4 copy-start.25
  199.3 3.4 copy-start.62
  203.0 3.6 copy-start.7
  208.9 6.6 %copy-start.26 = (f32[128,128]{1,0:T(8,128)S(1)}, f32[128,128]{1,0:T(8,128)}, u32[]{:S(2)}) copy-start(f32[128,128]{1,0:T(8,128)} %copy-done.25) | copy-start | bytes 196612
  208.9 6.6 %copy-start.28 = (bf16[128,128]{1,0:T(8,128)(2,1)S(1)}, bf16[128,128]{1,0:T(8,128)(2,1)}, u32[]{:S(2)}) copy-start(bf16[128,128]{1,0:T(8,128)(2,1)} %fusion.35) | copy-start | bytes 98308
  208.9 6.8 %copy-start.13 = (f32[2048,256]{1,0:T(8,128)S(1)}, f32[2048,256]{1,0:T(8,128)}, u32[]{:S(2)}) copy-start(f32[2048,256]{1,0:T(8,128)} %convolution_bitcast_fusion) | copy-start | bytes 6291460
  215.6 2.5 copy-start.20
  215.6 2.5 copy-start.37
  215.7 2.5 copy-start.42
  215.7 2.5 copy-start.48
  215.7 2.5 copy-start.50
  215.7 2.5 copy-start.51
  218.1 107.8 %reduce-scatter.10.cloned.1.call-start = ((), (), s32[]{:S(2)}) async-start(), calls=%async_computation.13 | async-start | bytes 2228224
  218.2 3.4 copy-start.2
  218.2 3.4 copy-start.6
  218.2 3.4 copy-start.21
  218.2 3.3 copy-start.35
  220.5 2.6 copy-start.30
  220.5 2.6 copy-start.47
  231.8 170.5 %reduce-scatter.8.cloned.1.call-start = ((), (), s32[]{:S(2)}) async-start(), calls=%async_computation.10 | async-start | bytes 278528 | tf_op jit(solution)/shard_map/reduce_scatter | solution.py:237
  241.2 241.1 %reduce-scatter.6.cloned.1.call-start = ((), (), s32[]{:S(2)}) async-start(), calls=%async_computation.9 | async-start | bytes 2228224 | tf_op jit(solution)/shard_map/reduce_scatter | solution.py:236
  241.2 2.9 copy-start.15
  241.3 2.9 copy-start.32
  241.3 2.9 copy-start.34
  241.3 2.9 copy-start.44
  241.3 2.9 copy-start.57
  245.8 8.7 %copy-start.10 = (f32[1,1,128,2048]{2,3,1,0:T(8,128)S(1)}, f32[1,1,128,2048]{2,3,1,0:T(8,128)}, u32[]{:S(2)}) copy-start(f32[1,1,128,2048]{2,3,1,0:T(8,128)} %copy.191) | copy-start | bytes 3145732
  245.8 8.7 %copy-start.39 = (f32[32,64]{1,0:T(8,128)S(1)}, f32[32,64]{1,0:T(8,128)}, u32[]{:S(2)}) copy-start(f32[32,64]{1,0:T(8,128)} %add.246) | copy-start | bytes 24580
  245.8 8.7 %copy-start.41 = (f32[32,64]{1,0:T(8,128)S(1)}, f32[32,64]{1,0:T(8,128)}, u32[]{:S(2)}) copy-start(f32[32,64]{1,0:T(8,128)} %slice.59) | copy-start | bytes 24580
  247.7 25.6 %all-to-all-start.1 = ((bf16[16,8,2048]{2,1,0:T(8,128)(2,1)}), bf16[16,8,2048]{2,1,0:T(8,128)(2,1)S(1)}, u32[]{:S(2)}, u32[]{:S(2)}) async-start(bf16[16,8,2048]{2,1,0:T(8,128)(2,1)} %copy.211), calls=%async_computation.1 | async-start | bytes 1048576 | tf_op jit(solution)/shard_map/all_to_all | solution.py:202
  257.4 2.8 copy-start.8
  257.4 4.1 copy-start.59
  257.4 4.1 copy-start.11
  261.5 11.9 %copy-start.12 = (f32[1,1,128,2048]{3,2,1,0:T(8,128)S(1)}, f32[1,1,128,2048]{3,2,1,0:T(8,128)}, u32[]{:S(2)}) copy-start(f32[1,1,128,2048]{3,2,1,0:T(8,128)} %copy.201) | copy-start | bytes 3145732
  262.6 64.3 %copy-start.54 = (f32[256]{0:T(256)S(1)}, f32[256]{0:T(256)}, u32[]{:S(2)}) copy-start(f32[256]{0:T(256)} %get-tuple-element.230) | copy-start | bytes 3076
  (11 other events, 15.2 us)
Sparse Core Ops, SparseCore 0:
  10.7 69.5 all-gather.6
  83.1 54.5 all-gather.8
  140.8 7.8 all-gather.12
  190.0 10.2 all-gather.10
  218.2 21.2 all-reduce.7
  241.7 84.2 reduce-scatter.9
  328.2 74.0 reduce-scatter.7
  404.5 77.7 reduce-scatter.5
where the time goes:
time: 493 us; the launch traced here: 491 us
  waiting for transfers between devices  279 us (57%)
  matrix products  49.4 us (10%)
  blocking collectives  48.2 us (10%)
  local copies, waits for them, and re-layouts  43.1 us (9%)
  other arithmetic  31.3 us (6%)
  starting transfers between devices  24 us (5%)
  between operations  15.8 us (3%)
    reduce_scatter x1, waiting for transfers between devices, per_device(): lax.psum_scatter(proj_sum, 'frame', scatter_dimension=0, tiled=True)  78.7 us
    reduce_scatter x1, waiting for transfers between devices, per_device(): lax.psum_scatter(step_sum, 'frame', scatter_dimension=0, tiled=True)  74.5 us
    unnamed x9, waiting for transfers between devices  51.6 us
    all_gather x1, waiting for transfers between devices, per_device(): lax.all_gather(proj_weight, 'frame', axis=0, tiled=True)  42.8 us
    all_gather x1, blocking collectives, per_device(): lax.all_gather(step_weight, 'frame', axis=0, tiled=True)  42 us
    dot_general x6, matrix products, block_parts(): jnp.einsum('shtu,suhp->sthp', weights, inputs, preferred_element_type=jnp...  17 us
    all_gather x1, waiting for transfers between devices, per_device(): mod_full = lax.all_gather(mod_weight, 'frame', axis=1, tiled=True)  12.4 us
    all_to_all x1, waiting for transfers between devices, per_device(): lax.all_to_all(time_low, 'frame', split_axis=0, concat_axis=0, tiled=True)  10.8 us
  transfers between devices with their start and end apart: 12, of which 7 were waited for; matrix products, arithmetic and copies ran while one was open for 25% of the time, Pallas kernels for 0%

commit v1 on v0

--- a/solution.py
+++ b/solution.py
@@ -124,6 +124,31 @@
     rate_time,
     skip_gain,
 ):
+
+    def _pass_unit(vals):
+        opened, extra, all_values = (lax.axis_size("frame"), lax.axis_index("frame"), vals.shape[0])
+        val2 = lax.dynamic_update_slice_in_dim(
+            jnp.zeros(
+                [tick * opened if it == 0 else tick for it, tick in enumerate(vals.shape)],
+                vals.dtype,
+            ),
+            vals,
+            extra * all_values,
+            axis=0,
+        )
+        known = r2 = vals
+        for kk in range(1, opened // 2 + 1):
+            known = lax.ppermute(known, "frame", [(it, (it + 1) % opened) for it in range(opened)])
+            val2 = lax.dynamic_update_slice_in_dim(
+                val2, known, (extra - kk) % opened * all_values, axis=0
+            )
+            if 2 * kk < opened:
+                r2 = lax.ppermute(r2, "frame", [(it, (it - 1) % opened) for it in range(opened)])
+                val2 = lax.dynamic_update_slice_in_dim(
+                    val2, r2, (extra + kk) % opened * all_values, axis=0
+                )
+        return val2
+
     frame_count = lax.axis_size("frame")
     row_count = lax.axis_size("row")
     frame_id = lax.axis_index("frame")
@@ -137,7 +162,7 @@
     factor = (frame_count * row_count * band_len) ** (-0.5)
     activated = time_embed(timestep, mod_weight.shape[0]).astype(jnp.bfloat16)
     proj_full, step_full = (
-        lax.all_gather(proj_weight, "frame", axis=0, tiled=True),
+        _pass_unit(proj_weight),
         lax.all_gather(step_weight, "frame", axis=0, tiled=True),
     )
     mod_full = lax.all_gather(mod_weight, "frame", axis=1, tiled=True)

time: 493 us -> 509 us (1.032)
  starting transfers between devices: 24 us -> 63.3 us
  waiting for transfers between devices: 279 us -> 251 us
  local copies, waits for them, and re-layouts: 43.1 us -> 49.9 us
    all_gather x1 -> x0, waiting for transfers between devices: 42.8 us -> none  [per_device(): lax.all_gather(proj_weight, 'frame', axis=0, tiled=True)]
    ppermute x0 -> x15, starting transfers between devices: none -> 38.2 us  [the longest x7 36.1 us: _pass_unit(): lax.ppermute(r2, 'frame', [(it, (it - 1) % opened) for it in range(opened)])]
    ppermute x0 -> x15, waiting for transfers between devices: none -> 26.1 us  [the longest x8 16.1 us: _pass_unit(): lax.ppermute(known, 'frame', [(it, (it + 1) % opened) for it in range(ope...]
    all_gather x1, waiting for transfers between devices: 12.4 us -> 0.01 us  [per_device(): mod_full = lax.all_gather(mod_weight, 'frame', axis=1, tiled=True)]
    unnamed x9 -> x8, waiting for transfers between devices: 51.6 us -> 51.6 us
  transfers between devices with their start and end apart: 12 -> 26, of which waited for: 7 -> 14; matrix products, arithmetic and copies ran while one was open for 25% -> 24% of each run, Pallas kernels for 0% -> 0%
where the time goes in v1:
time: 509 us; the launch traced here: 507 us
  waiting for transfers between devices  251 us (49%)
  starting transfers between devices  63.3 us (12%)
  local copies, waits for them, and re-layouts  49.9 us (10%)
  matrix products  48.6 us (10%)
  blocking collectives  47.5 us (9%)
  other arithmetic  30.3 us (6%)
  between operations  16.1 us (3%)
    reduce_scatter x1, waiting for transfers between devices, per_device(): lax.psum_scatter(proj_sum, 'frame', scatter_dimension=0, tiled=True)  78.7 us
    reduce_scatter x1, waiting for transfers between devices, per_device(): lax.psum_scatter(step_sum, 'frame', scatter_dimension=0, tiled=True)  74.5 us
    unnamed x8, waiting for transfers between devices  51.6 us
    all_gather x1, blocking collectives, per_device(): lax.all_gather(step_weight, 'frame', axis=0, tiled=True)  42.4 us
    ppermute x7, starting transfers between devices, _pass_unit(): lax.ppermute(r2, 'frame', [(it, (it - 1) % opened) for it in range(opened)])  36.1 us
    dot_general x6, matrix products, block_parts(): jnp.einsum('shtu,suhp->sthp', weights, inputs, preferred_element_type=jnp...  19.1 us
    ppermute x8, waiting for transfers between devices, _pass_unit(): lax.ppermute(known, 'frame', [(it, (it + 1) % opened) for it in range(ope...  16.1 us
    all_to_all x1, waiting for transfers between devices, per_device(): lax.all_to_all(time_low, 'frame', split_axis=0, concat_axis=0, tiled=True)  10.7 us
  transfers between devices with their start and end apart: 26, of which 14 were waited for; matrix products, arithmetic and copies ran while one was open for 24% of the time, Pallas kernels for 0%

profile of v1, /device:TPU:0, one launch (start us, length us, event | category | flops | bytes accessed | tf_op | source)
XLA Modules:
  0.0 506.7 jit_solution(9540948758815477897)
XLA Ops:
  7.9 7.0 %collective-permute-start.1 = (bf16[128,256]{1,0:T(8,128)(2,1)}, bf16[128,256]{1,0:T(8,128)(2,1)S(1)}, u32[]{:S(2)}, u32[]{:S(2)}) collective-permute-start(bf16[128,256]{1,0:T(8,128)(2,1)} %param.20), channel_id=1, source_target_pairs={{0,30},{2,0},{4,2},{6,4},{8,6},{10,8},{12,10},{14,12},{16,14},{18,... | collective-permute-start | bytes 196616 | tf_op jit(solution)/shard_map/ppermute | solution.py:146
  14.9 7.0 %all-to-all-start.2 = ((bf16[16,8,2048]{2,1,0:T(8,128)(2,1)}), bf16[16,8,2048]{2,1,0:T(8,128)(2,1)S(1)}, u32[]{:S(2)}, u32[]{:S(2)}) async-start(bf16[16,8,2048]{2,1,0:T(8,128)(2,1)} %bitcast.449), calls=%async_computation.2 | async-start | bytes 1048576 | tf_op jit(solution)/shard_map/all_to_all | solution.py:193
  27.6 42.4 %all_gather.25 = bf16[2048,32]{0,1:T(8,128)(2,1)S(1)} all-gather(bf16[128,32]{0,1:T(8,128)(2,1)S(1)} %copy-done.45), channel_id=1, replica_groups=mesh['frame'=16,'row'=2] {'frame'}, dimensions={0}, use_global_device_ids=true | all-gather | bytes 139264 | tf_op jit(solution)/shard_map/all_gather | solution.py:166
  70.0 2.0 collective-permute-start.2
  72.0 2.2 collective-permute-done.3
  74.2 5.1 collective-permute-start.5
  79.3 2.2 collective-permute-done.5
  81.5 6.1 %collective-permute-start.7 = (bf16[128,256]{1,0:T(8,128)(2,1)S(1)}, bf16[128,256]{1,0:T(8,128)(2,1)S(1)}, u32[]{:S(2)}, u32[]{:S(2)}) collective-permute-start(bf16[128,256]{1,0:T(8,128)(2,1)S(1)} %collective-permute-done.5), channel_id=1, source_target_pairs={{0,30},{2,0},{4,2},{6,4},{8,6},{10,8},{12,10},{14,12},{16,14},{18,... | collective-permute-start | bytes 196616 | tf_op jit(solution)/shard_map/ppermute | solution.py:146
  87.6 1.9 collective-permute-done.7
  89.5 6.1 %collective-permute-start.9 = (bf16[128,256]{1,0:T(8,128)(2,1)S(1)}, bf16[128,256]{1,0:T(8,128)(2,1)S(1)}, u32[]{:S(2)}, u32[]{:S(2)}) collective-permute-start(bf16[128,256]{1,0:T(8,128)(2,1)S(1)} %collective-permute-done.7), channel_id=1, source_target_pairs={{0,30},{2,0},{4,2},{6,4},{8,6},{10,8},{12,10},{14,12},{16,14},{18,... | collective-permute-start | bytes 196616 | tf_op jit(solution)/shard_map/ppermute | solution.py:146
  95.6 1.9 collective-permute-done.9
  97.5 6.0 %collective-permute-start.11 = (bf16[128,256]{1,0:T(8,128)(2,1)S(1)}, bf16[128,256]{1,0:T(8,128)(2,1)S(1)}, u32[]{:S(2)}, u32[]{:S(2)}) collective-permute-start(bf16[128,256]{1,0:T(8,128)(2,1)S(1)} %collective-permute-done.9), channel_id=1, source_target_pairs={{0,30},{2,0},{4,2},{6,4},{8,6},{10,8},{12,10},{14,12},{16,14},{18,... | collective-permute-start | bytes 196616 | tf_op jit(solution)/shard_map/ppermute | solution.py:146
  103.5 1.9 collective-permute-done.11
  105.3 6.0 %collective-permute-start.13 = (bf16[128,256]{1,0:T(8,128)(2,1)S(1)}, bf16[128,256]{1,0:T(8,128)(2,1)S(1)}, u32[]{:S(2)}, u32[]{:S(2)}) collective-permute-start(bf16[128,256]{1,0:T(8,128)(2,1)S(1)} %collective-permute-done.11), channel_id=1, source_target_pairs={{0,30},{2,0},{4,2},{6,4},{8,6},{10,8},{12,10},{14,12},{16,14},{18,... | collective-permute-start | bytes 196616 | tf_op jit(solution)/shard_map/ppermute | solution.py:146
  111.8 7.8 %collective-permute-done.12 = bf16[128,256]{1,0:T(8,128)(2,1)S(1)} collective-permute-done((bf16[128,256]{1,0:T(8,128)(2,1)S(1)}, bf16[128,256]{1,0:T(8,128)(2,1)S(1)}, u32[]{:S(2)}, u32[]{:S(2)}) %collective-permute-start.12) | collective-permute-done | bytes 65568 | tf_op jit(solution)/shard_map/ppermute | solution.py:141
  119.6 7.8 %collective-permute-done.14 = bf16[128,256]{1,0:T(8,128)(2,1)S(1)} collective-permute-done((bf16[128,256]{1,0:T(8,128)(2,1)S(1)}, bf16[128,256]{1,0:T(8,128)(2,1)S(1)}, u32[]{:S(2)}, u32[]{:S(2)}) %collective-permute-start.14) | collective-permute-done | bytes 65568 | tf_op jit(solution)/shard_map/ppermute | solution.py:141
  127.5 2.1 reshape.933
  129.5 2.0 fusion.186
  132.3 1.8 all_gather.26
  135.9 3.6 all-to-all-start
  140.8 2.5 copy.213
  143.3 2.8 convert_multiply_fusion
  146.1 2.6 copy.223
  148.8 2.5 copy.214
  152.6 1.4 convolution_convert_fusion.5
  155.7 2.0 reshape.936
  158.2 4.1 convert_bitcast_fusion
  162.3 4.5 fusion.28
  168.1 3.6 copy.231
  171.7 2.8 reshape.922
  175.8 1.6 fusion.5
  177.4 6.8 %all-to-all-start.3 = ((bf16[16,8,2048]{2,1,0:T(8,128)(2,1)}), bf16[16,8,2048]{2,1,0:T(8,128)(2,1)}, u32[]{:S(2)}, u32[]{:S(2)}) async-start(bf16[16,8,2048]{2,1,0:T(8,128)(2,1)} %fusion.5), calls=%async_computation.3 | async-start | bytes 1048576 | tf_op jit(solution)/shard_map/all_to_all | solution.py:228
  184.4 1.4 while.28
  185.8 2.5 multiply_reduce_fusion.2
  190.8 2.5 copy.197
  193.4 2.3 fusion.52
  198.4 2.7 convolution_bitcast_fusion
  202.9 1.5 copy.200
  204.5 4.1 fusion.26
  213.2 2.4 fusion.37
  215.6 2.3 multiply_reduce_fusion.1
  218.0 1.6 copy.224
  223.4 1.6 bitcast_add_fusion
  225.0 2.6 reduce_window_sum.49
  229.2 2.0 fusion.6
  232.2 2.4 fusion
  234.7 2.3 fusion.34
  238.3 3.0 fusion.72
  241.3 3.4 psum.23
  244.7 1.8 copy.246
  246.6 9.2 %all-reduce.8.cloned.1.call-done = (bf16[2048,256]{1,0:T(8,128)(2,1)}, bf16[2048,32]{0,1:T(8,128)(2,1)}) async-done(((bf16[2048,256]{1,0:T(8,128)(2,1)}, bf16[2048,32]{0,1:T(8,128)(2,1)}), (bf16[2048,256]{1,0:T(8,128)(2,1)}, bf16[2048,32]{0,1:T(8,128)(2,1)})) %all-reduce.8.cloned.1.call-update) | async-done | bytes 1179664 | tf_op jit(solution)/shard_map/psum | solution.py:256
  255.7 1.6 convert_element_type.535
  257.7 2.8 convert_element_type.533
  260.6 1.3 fusion.29
  264.2 6.8 %all-to-all-start.1 = ((bf16[16,8,2048]{2,1,0:T(8,128)(2,1)}), bf16[16,8,2048]{2,1,0:T(8,128)(2,1)S(1)}, u32[]{:S(2)}, u32[]{:S(2)}) async-start(bf16[16,8,2048]{2,1,0:T(8,128)(2,1)} %copy.211), calls=%async_computation.1 | async-start | bytes 1048576 | tf_op jit(solution)/shard_map/all_to_all | solution.py:227
  271.0 2.8 fusion.82
  273.8 1.6 copy.201
  275.5 1.4 copy.202
  276.8 2.4 fusion.83
  279.2 10.7 %all-to-all-done.1 = bf16[16,8,2048]{2,1,0:T(8,128)(2,1)S(1)} async-done(((bf16[16,8,2048]{2,1,0:T(8,128)(2,1)}), bf16[16,8,2048]{2,1,0:T(8,128)(2,1)S(1)}, u32[]{:S(2)}, u32[]{:S(2)}) %all-to-all-start.1) | async-done | bytes 524320 | tf_op jit(solution)/shard_map/all_to_all | solution.py:227
  291.1 50.8 %reduce-scatter.10.cloned.1.call-done = f32[256,1]{1,0:T(8,128)} async-done(((f32[4096,1]{1,0:T(8,128)}), f32[256,1]{1,0:T(8,128)}) %reduce-scatter.10.cloned.1.call-update) | async-done | bytes 1040
  343.7 74.5 %reduce-scatter.8.cloned.1.call-done = f32[128,32]{0,1:T(8,128)} async-done(((f32[2048,32]{0,1:T(8,128)}), f32[128,32]{0,1:T(8,128)}) %reduce-scatter.8.cloned.1.call-update) | async-done | bytes 16400 | tf_op jit(solution)/shard_map/reduce_scatter | solution.py:262
  419.5 78.7 %reduce-scatter.6.cloned.1.call-done = f32[128,256]{1,0:T(8,128)} async-done(((f32[2048,256]{1,0:T(8,128)}), f32[128,256]{1,0:T(8,128)}) %reduce-scatter.6.cloned.1.call-update) | async-done | bytes 131088 | tf_op jit(solution)/shard_map/reduce_scatter | solution.py:261
  498.3 1.6 broadcast_multiply_fusion
  (245 shorter events, 43.6 us)
Async XLA Ops:
  7.2 17.0 %copy-start.35 = (bf16[128,256]{1,0:T(8,128)(2,1)S(1)}, bf16[128,256]{1,0:T(8,128)(2,1)}, u32[]{:S(2)}) copy-start(bf16[128,256]{1,0:T(8,128)(2,1)} %param.20) | copy-start | bytes 196612
  7.2 17.3 %copy-start.5 = (bf16[1,1,128,2048]{3,2,1,0:T(8,128)(2,1)S(1)}, bf16[1,1,128,2048]{3,2,1,0:T(8,128)(2,1)}, u32[]{:S(2)}) copy-start(bf16[1,1,128,2048]{3,2,1,0:T(8,128)(2,1)} %param.17) | copy-start | bytes 1572868
  7.2 17.1 %copy-start = (bf16[1,1,128,2048]{3,2,1,0:T(8,128)(2,1)S(1)}, bf16[1,1,128,2048]{3,2,1,0:T(8,128)(2,1)}, u32[]{:S(2)}) copy-start(bf16[1,1,128,2048]{3,2,1,0:T(8,128)(2,1)} %param.16) | copy-start | bytes 1572868
  7.2 122.3 %all-gather.6.cloned.1.call-start = ((), (), s32[]{:S(2)}) async-start(), calls=%async_computation.7 | async-start | bytes 2228224 | tf_op jit(solution)/shard_map/all_gather | solution.py:168
  7.9 62.0 %collective-permute-start.1 = (bf16[128,256]{1,0:T(8,128)(2,1)}, bf16[128,256]{1,0:T(8,128)(2,1)S(1)}, u32[]{:S(2)}, u32[]{:S(2)}) collective-permute-start(bf16[128,256]{1,0:T(8,128)(2,1)} %param.20), channel_id=1, source_target_pairs={{0,30},{2,0},{4,2},{6,4},{8,6},{10,8},{12,10},{14,12},{16,14},{18,... | collective-permute-start | bytes 196616 | tf_op jit(solution)/shard_map/ppermute | solution.py:146
  14.9 55.0 %collective-permute-start = (bf16[128,256]{1,0:T(8,128)(2,1)}, bf16[128,256]{1,0:T(8,128)(2,1)S(1)}, u32[]{:S(2)}, u32[]{:S(2)}) collective-permute-start(bf16[128,256]{1,0:T(8,128)(2,1)} %param.20), channel_id=1, source_target_pairs={{0,2},{2,4},{4,6},{6,8},{8,10},{10,12},{12,14},{14,16},{16,18},{18... | collective-permute-start | bytes 196616 | tf_op jit(solution)/shard_map/ppermute | solution.py:141
  14.9 112.5 %all-to-all-start.2 = ((bf16[16,8,2048]{2,1,0:T(8,128)(2,1)}), bf16[16,8,2048]{2,1,0:T(8,128)(2,1)S(1)}, u32[]{:S(2)}, u32[]{:S(2)}) async-start(bf16[16,8,2048]{2,1,0:T(8,128)(2,1)} %bitcast.449), calls=%async_computation.2 | async-start | bytes 1048576 | tf_op jit(solution)/shard_map/all_to_all | solution.py:193
  23.5 134.7 %copy-start.51 = (pred[16,16]{1,0:T(8,128)(4,1)}, pred[16,16]{1,0:T(8,128)(4,1)S(1)}, u32[]{:S(2)}) copy-start(pred[16,16]{1,0:T(8,128)(4,1)S(1)} %iota_compare_fusion.1) | copy-start | bytes 772
  24.1 2.7 copy-start.55
  24.1 3.4 copy-start.45
  24.5 168.9 %copy-start.39 = (f32[128]{0:T(128)}, f32[128]{0:T(128)S(1)}, u32[]{:S(2)}) copy-start(f32[128]{0:T(128)S(1)} %fusion.162) | copy-start | bytes 1540
  70.0 4.3 collective-permute-start.3
  70.0 9.3 %collective-permute-start.2 = (bf16[128,256]{1,0:T(8,128)(2,1)S(1)}, bf16[128,256]{1,0:T(8,128)(2,1)S(1)}, u32[]{:S(2)}, u32[]{:S(2)}) collective-permute-start(bf16[128,256]{1,0:T(8,128)(2,1)S(1)} %collective-permute-done), channel_id=1, source_target_pairs={{0,2},{2,4},{4,6},{6,8},{8,10},{10,12},{12,14},{14,16},{16,18},{18... | collective-permute-start | bytes 196616 | tf_op jit(solution)/shard_map/ppermute | solution.py:141
  74.2 7.3 %collective-permute-start.5 = (bf16[128,256]{1,0:T(8,128)(2,1)S(1)}, bf16[128,256]{1,0:T(8,128)(2,1)S(1)}, u32[]{:S(2)}, u32[]{:S(2)}) collective-permute-start(bf16[128,256]{1,0:T(8,128)(2,1)S(1)} %collective-permute-done.3), channel_id=1, source_target_pairs={{0,30},{2,0},{4,2},{6,4},{8,6},{10,8},{12,10},{14,12},{16,14},{18,... | collective-permute-start | bytes 196616 | tf_op jit(solution)/shard_map/ppermute | solution.py:146
  79.3 8.3 %collective-permute-start.4 = (bf16[128,256]{1,0:T(8,128)(2,1)S(1)}, bf16[128,256]{1,0:T(8,128)(2,1)S(1)}, u32[]{:S(2)}, u32[]{:S(2)}) collective-permute-start(bf16[128,256]{1,0:T(8,128)(2,1)S(1)} %collective-permute-done.2), channel_id=1, source_target_pairs={{0,2},{2,4},{4,6},{6,8},{8,10},{10,12},{12,14},{14,16},{16,18},{18... | collective-permute-start | bytes 196616 | tf_op jit(solution)/shard_map/ppermute | solution.py:141
  81.5 8.0 %collective-permute-start.7 = (bf16[128,256]{1,0:T(8,128)(2,1)S(1)}, bf16[128,256]{1,0:T(8,128)(2,1)S(1)}, u32[]{:S(2)}, u32[]{:S(2)}) collective-permute-start(bf16[128,256]{1,0:T(8,128)(2,1)S(1)} %collective-permute-done.5), channel_id=1, source_target_pairs={{0,30},{2,0},{4,2},{6,4},{8,6},{10,8},{12,10},{14,12},{16,14},{18,... | collective-permute-start | bytes 196616 | tf_op jit(solution)/shard_map/ppermute | solution.py:146
  87.6 8.0 %collective-permute-start.6 = (bf16[128,256]{1,0:T(8,128)(2,1)S(1)}, bf16[128,256]{1,0:T(8,128)(2,1)S(1)}, u32[]{:S(2)}, u32[]{:S(2)}) collective-permute-start(bf16[128,256]{1,0:T(8,128)(2,1)S(1)} %collective-permute-done.4), channel_id=1, source_target_pairs={{0,2},{2,4},{4,6},{6,8},{8,10},{10,12},{12,14},{14,16},{16,18},{18... | collective-permute-start | bytes 196616 | tf_op jit(solution)/shard_map/ppermute | solution.py:141
  89.5 8.0 %collective-permute-start.9 = (bf16[128,256]{1,0:T(8,128)(2,1)S(1)}, bf16[128,256]{1,0:T(8,128)(2,1)S(1)}, u32[]{:S(2)}, u32[]{:S(2)}) collective-permute-start(bf16[128,256]{1,0:T(8,128)(2,1)S(1)} %collective-permute-done.7), channel_id=1, source_target_pairs={{0,30},{2,0},{4,2},{6,4},{8,6},{10,8},{12,10},{14,12},{16,14},{18,... | collective-permute-start | bytes 196616 | tf_op jit(solution)/shard_map/ppermute | solution.py:146
  95.6 7.9 %collective-permute-start.8 = (bf16[128,256]{1,0:T(8,128)(2,1)S(1)}, bf16[128,256]{1,0:T(8,128)(2,1)S(1)}, u32[]{:S(2)}, u32[]{:S(2)}) collective-permute-start(bf16[128,256]{1,0:T(8,128)(2,1)S(1)} %collective-permute-done.6), channel_id=1, source_target_pairs={{0,2},{2,4},{4,6},{6,8},{8,10},{10,12},{12,14},{14,16},{16,18},{18... | collective-permute-start | bytes 196616 | tf_op jit(solution)/shard_map/ppermute | solution.py:141
  97.5 7.9 %collective-permute-start.11 = (bf16[128,256]{1,0:T(8,128)(2,1)S(1)}, bf16[128,256]{1,0:T(8,128)(2,1)S(1)}, u32[]{:S(2)}, u32[]{:S(2)}) collective-permute-start(bf16[128,256]{1,0:T(8,128)(2,1)S(1)} %collective-permute-done.9), channel_id=1, source_target_pairs={{0,30},{2,0},{4,2},{6,4},{8,6},{10,8},{12,10},{14,12},{16,14},{18,... | collective-permute-start | bytes 196616 | tf_op jit(solution)/shard_map/ppermute | solution.py:146
  103.4 8.3 %collective-permute-start.10 = (bf16[128,256]{1,0:T(8,128)(2,1)S(1)}, bf16[128,256]{1,0:T(8,128)(2,1)S(1)}, u32[]{:S(2)}, u32[]{:S(2)}) collective-permute-start(bf16[128,256]{1,0:T(8,128)(2,1)S(1)} %collective-permute-done.8), channel_id=1, source_target_pairs={{0,2},{2,4},{4,6},{6,8},{8,10},{10,12},{12,14},{14,16},{16,18},{18... | collective-permute-start | bytes 196616 | tf_op jit(solution)/shard_map/ppermute | solution.py:141
  105.3 14.3 %collective-permute-start.13 = (bf16[128,256]{1,0:T(8,128)(2,1)S(1)}, bf16[128,256]{1,0:T(8,128)(2,1)S(1)}, u32[]{:S(2)}, u32[]{:S(2)}) collective-permute-start(bf16[128,256]{1,0:T(8,128)(2,1)S(1)} %collective-permute-done.11), channel_id=1, source_target_pairs={{0,30},{2,0},{4,2},{6,4},{8,6},{10,8},{12,10},{14,12},{16,14},{18,... | collective-permute-start | bytes 196616 | tf_op jit(solution)/shard_map/ppermute | solution.py:146
  111.7 7.9 %collective-permute-start.12 = (bf16[128,256]{1,0:T(8,128)(2,1)S(1)}, bf16[128,256]{1,0:T(8,128)(2,1)S(1)}, u32[]{:S(2)}, u32[]{:S(2)}) collective-permute-start(bf16[128,256]{1,0:T(8,128)(2,1)S(1)} %collective-permute-done.10), channel_id=1, source_target_pairs={{0,2},{2,4},{4,6},{6,8},{8,10},{10,12},{12,14},{14,16},{16,18},{18... | collective-permute-start | bytes 196616 | tf_op jit(solution)/shard_map/ppermute | solution.py:141
  111.8 19.9 %copy-start.46 = (f32[32]{0:T(128)S(1)}, f32[32]{0:T(128)}, u32[]{:S(2)}) copy-start(f32[32]{0:T(128)} %param.22) | copy-start | bytes 388
  119.6 7.9 %collective-permute-start.14 = (bf16[128,256]{1,0:T(8,128)(2,1)S(1)}, bf16[128,256]{1,0:T(8,128)(2,1)S(1)}, u32[]{:S(2)}, u32[]{:S(2)}) collective-permute-start(bf16[128,256]{1,0:T(8,128)(2,1)S(1)} %collective-permute-done.12), channel_id=1, source_target_pairs={{0,2},{2,4},{4,6},{6,8},{8,10},{10,12},{12,14},{14,16},{16,18},{18... | collective-permute-start | bytes 196616 | tf_op jit(solution)/shard_map/ppermute | solution.py:141
  127.5 47.6 %copy-start.1 = (bf16[2048,256]{1,0:T(8,128)(2,1)}, bf16[2048,256]{1,0:T(8,128)(2,1)S(1)}, u32[]{:S(2)}) copy-start(bf16[2048,256]{1,0:T(8,128)(2,1)S(1)} %constant_dynamic-update-slice_fusion) | copy-start | bytes 3145732
  131.6 54.2 %copy-start.31 = (f32[32,64]{1,0:T(8,128)}, f32[32,64]{1,0:T(8,128)S(1)}, u32[]{:S(2)}) copy-start(f32[32,64]{1,0:T(8,128)S(1)} %slice.59) | copy-start | bytes 24580
  131.7 54.1 %copy-start.33 = (f32[32,64]{1,0:T(8,128)}, f32[32,64]{1,0:T(8,128)S(1)}, u32[]{:S(2)}) copy-start(f32[32,64]{1,0:T(8,128)S(1)} %add.369) | copy-start | bytes 24580
  132.3 56.1 %copy-start.50 = (f32[32]{0:T(128)}, f32[32]{0:T(128)S(1)}, u32[]{:S(2)}) copy-start(f32[32]{0:T(128)S(1)} %get-tuple-element.241) | copy-start | bytes 388
  135.9 19.0 %all-to-all-start = ((bf16[16,8,2048]{2,1,0:T(8,128)(2,1)}), bf16[16,8,2048]{2,1,0:T(8,128)(2,1)S(1)}, u32[]{:S(2)}, u32[]{:S(2)}) async-start(bf16[16,8,2048]{2,1,0:T(8,128)(2,1)} %fusion.64), calls=%async_computation | async-start | bytes 1048576 | tf_op jit(solution)/shard_map/all_to_all | solution.py:192
  139.5 44.8 %all-gather.10.cloned.1.call-start = ((), (), s32[]{:S(2)}) async-start(), calls=%async_computation.11 | async-start | bytes 1572864 | tf_op jit(solution)/shard_map/all_gather | solution.py:35
  151.7 3.8 copy-start.48
  155.5 6.8 %copy-start.21 = (f32[8,32,16]{2,1,0:T(8,128)}, f32[8,32,16]{2,1,0:T(8,128)S(1)}, u32[]{:S(2)}) copy-start(f32[8,32,16]{2,1,0:T(8,128)S(1)} %copy.208) | copy-start | bytes 49156
  158.2 4.1 copy-start.37
  158.2 4.1 copy-start.12
  158.2 4.1 copy-start.14
  174.7 2.8 copy-start.19
  175.8 8.6 %copy-start.56 = (bf16[2,1,32]{2,1,0:T(2,128)(2,1)S(1)}, bf16[2,1,32]{2,1,0:T(2,128)(2,1)}, u32[]{:S(2)}) copy-start(bf16[2,1,32]{2,1,0:T(2,128)(2,1)} %all_gather.26) | copy-start | bytes 388
  177.4 60.9 %all-to-all-start.3 = ((bf16[16,8,2048]{2,1,0:T(8,128)(2,1)}), bf16[16,8,2048]{2,1,0:T(8,128)(2,1)}, u32[]{:S(2)}, u32[]{:S(2)}) async-start(bf16[16,8,2048]{2,1,0:T(8,128)(2,1)} %fusion.5), calls=%async_computation.3 | async-start | bytes 1048576 | tf_op jit(solution)/shard_map/all_to_all | solution.py:228
  184.2 27.6 %all-gather.8.cloned.1.call-start = ((), (), s32[]{:S(2)}) async-start(), calls=%async_computation.10 | async-start | bytes 1572864 | tf_op jit(solution)/shard_map/all_gather | solution.py:13
  189.8 3.6 copy-start.28
  198.1 57.6 %all-reduce.8.cloned.1.call-start = ((), (), s32[]{:S(2)}) async-start(), calls=%async_computation.13 | async-start | bytes 2359296 | tf_op jit(solution)/shard_map/psum | solution.py:256
  198.4 2.7 copy-start.17
  202.9 5.6 %copy-start.42 = (f32[32,128]{1,0:T(8,128)}, f32[32,128]{1,0:T(8,128)S(1)}, u32[]{:S(2)}) copy-start(f32[32,128]{1,0:T(8,128)S(1)} %copy.195) | copy-start | bytes 49156
  208.5 3.3 copy-start.20
  212.0 3.6 copy-start.7
  212.0 3.6 copy-start.30
  218.0 14.1 %copy-start.11 = (f32[2048,256]{1,0:T(8,128)S(1)}, f32[2048,256]{1,0:T(8,128)}, u32[]{:S(2)}) copy-start(f32[2048,256]{1,0:T(8,128)} %convolution_bitcast_fusion) | copy-start | bytes 6291460
  234.6 107.4 %reduce-scatter.10.cloned.1.call-start = ((), (), s32[]{:S(2)}) async-start(), calls=%async_computation.12 | async-start | bytes 2228224
  234.7 3.3 copy-start.26
  246.5 171.7 %reduce-scatter.8.cloned.1.call-start = ((), (), s32[]{:S(2)}) async-start(), calls=%async_computation.9 | async-start | bytes 278528 | tf_op jit(solution)/shard_map/reduce_scatter | solution.py:262
  257.4 240.9 %reduce-scatter.6.cloned.1.call-start = ((), (), s32[]{:S(2)}) async-start(), calls=%async_computation.8 | async-start | bytes 2228224 | tf_op jit(solution)/shard_map/reduce_scatter | solution.py:261
  257.7 2.9 copy-start.13
  257.7 2.9 copy-start.22
  257.7 2.9 copy-start.24
  257.7 2.9 copy-start.38
  257.7 2.9 copy-start.52
  262.2 8.7 %copy-start.9 = (f32[1,1,128,2048]{2,3,1,0:T(8,128)S(1)}, f32[1,1,128,2048]{2,3,1,0:T(8,128)}, u32[]{:S(2)}) copy-start(f32[1,1,128,2048]{2,3,1,0:T(8,128)} %copy.191) | copy-start | bytes 3145732
  262.2 8.7 %copy-start.32 = (f32[32,64]{1,0:T(8,128)S(1)}, f32[32,64]{1,0:T(8,128)}, u32[]{:S(2)}) copy-start(f32[32,64]{1,0:T(8,128)} %copy-done.31) | copy-start | bytes 24580
  262.2 8.7 %copy-start.34 = (f32[32,64]{1,0:T(8,128)S(1)}, f32[32,64]{1,0:T(8,128)}, u32[]{:S(2)}) copy-start(f32[32,64]{1,0:T(8,128)} %copy-done.33) | copy-start | bytes 24580
  264.2 25.8 %all-to-all-start.1 = ((bf16[16,8,2048]{2,1,0:T(8,128)(2,1)}), bf16[16,8,2048]{2,1,0:T(8,128)(2,1)S(1)}, u32[]{:S(2)}, u32[]{:S(2)}) async-start(bf16[16,8,2048]{2,1,0:T(8,128)(2,1)} %copy.211), calls=%async_computation.1 | async-start | bytes 1048576 | tf_op jit(solution)/shard_map/all_to_all | solution.py:227
  273.8 3.0 copy-start.54
  276.8 13.1 %copy-start.10 = (f32[1,1,128,2048]{3,2,1,0:T(8,128)S(1)}, f32[1,1,128,2048]{3,2,1,0:T(8,128)}, u32[]{:S(2)}) copy-start(f32[1,1,128,2048]{3,2,1,0:T(8,128)} %copy.202) | copy-start | bytes 3145732
  279.2 63.7 %copy-start.47 = (f32[256]{0:T(256)S(1)}, f32[256]{0:T(256)}, u32[]{:S(2)}) copy-start(f32[256]{0:T(256)} %get-tuple-element.230) | copy-start | bytes 3076
  (19 other events, 34.5 us)
Sparse Core Ops, SparseCore 0:
  10.7 73.3 all-gather.5
  154.1 10.2 all-gather.9
  198.2 10.2 all-gather.7
  234.7 20.9 all-reduce.7
  257.8 84.0 reduce-scatter.9
  344.0 74.1 reduce-scatter.7
  420.5 77.7 reduce-scatter.5
